TPU v7x, 256 devices: a whole 4x4x8 slice. The times are simulated.
256 devices in a mesh: blk: 32 (over z, y_hi, core), cls: 8 (over x, y_lo).
Axes of the slice: x: 4, y: 4 (y_hi: 2, y_lo: 2; y = y_hi * 2 + y_lo), z: 8, core: 2. Of those that a mesh axis runs over, the one named last changes fastest.
Arguments:
- features: bfloat16 [2048, 2048], P('blk'), may hold values from -6 to 6
- labels: int32 [2048], P('blk'), may hold values from 0 to 655359
- offset: int32 [1], replicated, may hold values from 0 to 524288
- other_lse: float32 [2048], replicated, may hold values from 15 to 20
- weight: bfloat16 [131072, 2048], P(('blk', 'cls'))
- accum: float32 [131072, 2048], P(('blk', 'cls')), may hold values from 0.1 to 1
Outputs:
- new_weight: bfloat16 [131072, 2048], P(('blk', 'cls'))
- new_accum: float32 [131072, 2048], P(('blk', 'cls'))
- lse: float32 [2048], P('blk')
All inputs are finite; a program needn't handle non-finite values.
Results may differ from a plain program's by a relative error of at most 0.004.
Values may be sent and summed in bfloat16 or wider, within the bound.
A program may use at most 128 MiB of HBM per device.

v0:
```python
import jax
import jax.numpy as jnp
from jax import lax
from jax.sharding import PartitionSpec as P


def scores(rows, weight):
    return lax.dot_general(
        rows, weight, (((1,), (1,)), ((), ())), preferred_element_type=jnp.float32
    )


def gradient_term(logits, lse_rows, label_rows, first_class, rows):
    width = logits.shape[1]
    local = label_rows - first_class
    onehot = (local[:, None] == jnp.arange(width, dtype=jnp.int32)[None, :]).astype(jnp.float32)
    delta = (jnp.exp(logits - lse_rows[:, None]) - onehot).astype(jnp.bfloat16)
    return lax.dot_general(
        delta, rows, (((0,), (0,)), ((), ())), preferred_element_type=jnp.float32
    )


def body(features, labels, offset, other_lse, weight, accum):
    block = features.shape[0]
    cls_dev = weight.shape[0]
    device_rank = lax.axis_index("blk") * lax.axis_size("cls") + lax.axis_index("cls")
    first_class = offset[0] + device_rank * cls_dev
    all_rows, all_labels = (
        lax.all_gather(features, "blk", axis=0, tiled=True),
        lax.all_gather(labels, "blk", axis=0, tiled=True),
    )
    logits = scores(all_rows, weight)
    local_top = jnp.max(logits, axis=1)
    top = lax.pmax(local_top, ("blk", "cls"))
    total = lax.psum(jnp.sum(jnp.exp(logits - top[:, None]), axis=1), ("blk", "cls"))
    slab_lse = top + jnp.log(total)
    high = jnp.maximum(slab_lse, other_lse)
    lse = high + jnp.log(jnp.exp(slab_lse - high) + jnp.exp(other_lse - high))
    grad = gradient_term(logits, lse, all_labels, first_class, all_rows)
    new_accum = accum + grad * grad
    new_weight = (weight.astype(jnp.float32) - 0.05 * grad / (jnp.sqrt(new_accum) + 1e-10)).astype(
        jnp.bfloat16
    )
    own_lse = lax.dynamic_slice_in_dim(lse, lax.axis_index("blk") * block, block, 0)
    return (new_weight, new_accum, own_lse)


def solution(mesh):
    in_specs = (
        P("blk", None),
        P("blk"),
        P(),
        P(),
        P(("blk", "cls"), None),
        P(("blk", "cls"), None),
    )
    out_specs = (P(("blk", "cls"), None), P(("blk", "cls"), None), P("blk"))
    return jax.shard_map(body, mesh=mesh, in_specs=in_specs, out_specs=out_specs, check_vma=False)
```

profile of v0, /device:TPU:1, one launch (start us, length us, event | category | flops | bytes accessed | tf_op | source)
XLA Modules:
  0.0 299.9 jit_solution(17665709030679258281)
XLA Ops:
  7.2 0.0 all-gather.2.cloned.1.call-start
  7.2 0.7 all-gather.2.cloned.1.call-update
  8.6 1.3 dynamic-slice
  10.5 0.9 dynamic-update-slice
  11.4 18.9 %all-reduce = s32[2048]{0:T(1024)S(1)} all-reduce(s32[2048]{0:T(1024)S(1)} %dynamic-update-slice), channel_id=1, replica_groups=mesh['blk'=32,'cls'=8] {'blk'}, use_global_device_ids=true, to_apply=%add | all-reduce | flops 2048 | bytes 16384
  30.2 86.2 %all-gather.2.cloned.1.call-done = bf16[2048,2048]{1,0:T(8,128)(2,1)} async-done(((bf16[64,2048]{1,0:T(8,128)(2,1)}), bf16[2048,2048]{1,0:T(8,128)(2,1)}) %all-gather.2.cloned.1.call-update) | async-done | bytes 8388624 | tf_op jit(solution)/shard_map/all_gather | solution.py:29
  116.5 10.5 %fusion.4 = (f32[2048]{0:T(1024)S(1)}, f32[2048,512]{0,1:T(8,128)}) fusion(bf16[2048,2048]{1,0:T(8,128)(2,1)} %all-gather.2.cloned.1.call-done, bf16[512,2048]{1,0:T(8,128)(2,1)} %param.10), kind=kOutput, calls=%fused_computation.12 | convolution fusion | flops 4296013824 | bytes 14688256 | tf_op jit(solution)/shard_map/dot_general | solution.py:8
  127.0 0.0 copy-start
  127.0 0.0 copy-start.1
  127.0 74.8 %pmax.7 = f32[2048]{0:T(1024)S(1)} all-reduce(f32[2048]{0:T(1024)S(1)} %get-tuple-element.5), channel_id=1, replica_groups=mesh['blk'=32,'cls'=8] {'blk','cls'}, use_global_device_ids=true, to_apply=%region_1.0 | all-reduce | flops 2048 | bytes 16384 | tf_op jit(solution)/shard_map/pmax | solution.py:34
  201.8 2.8 exponential_reduce_fusion
  204.5 73.3 %psum.7 = f32[2048]{0:T(1024)S(1)} all-reduce(f32[2048]{0:T(1024)S(1)} %exponential_reduce_fusion), channel_id=1, replica_groups=mesh['blk'=32,'cls'=8] {'blk','cls'}, use_global_device_ids=true, to_apply=%region_3.0 | all-reduce | flops 2048 | bytes 16384 | tf_op jit(solution)/shard_map/psum | solution.py:35
  277.8 0.0 copy-done
  277.9 0.6 dynamic_slice.3
  278.5 0.0 copy-done.1
  278.5 14.6 %subtract_convert_fusion = (bf16[512,2048]{1,0:T(8,128)(2,1)}, f32[512,2048]{1,0:T(8,128)}) fusion(bf16[512,2048]{1,0:T(8,128)(2,1)S(1)} %copy-done.1, f32[512,2048]{1,0:T(8,128)} %param.11, bf16[2048,2048]{1,0:T(8,128)(2,1)} %all-gather.2.cloned.1.call-done, f32[2048,512]{0,1:T(8,128)} %get-tuple-element.6, s32[2048]{0:T(1024)S(1)} %broadcast_subtract_fusion, ...), kind=kOutput, calls=%fused_computation | convolution fusion | flops 4308598784 | bytes 25182208 | tf_op jit(solution)/shard_map/dot_general | solution.py:18
  (3 shorter events, 0.0 us)
Async XLA Ops:
  7.2 109.3 %all-gather.2.cloned.1.call-start = ((), (), s32[]{:S(2)}) async-start(), calls=%async_computation | async-start | bytes 8650752 | tf_op jit(solution)/shard_map/all_gather | solution.py:29
  127.0 150.9 %copy-start = (f32[2048]{0:T(1024)S(1)}, f32[2048]{0:T(1024)}, u32[]{:S(2)}) copy-start(f32[2048]{0:T(1024)} %param.9) | copy-start | bytes 24580
  127.0 151.5 %copy-start.1 = (bf16[512,2048]{1,0:T(8,128)(2,1)S(1)}, bf16[512,2048]{1,0:T(8,128)(2,1)}, u32[]{:S(2)}) copy-start(bf16[512,2048]{1,0:T(8,128)(2,1)} %param.10) | copy-start | bytes 6291460
Sparse Core Ops, SparseCore 0:
  10.8 105.6 all-gather.1
where the time goes:
time: 300 us
  blocking collectives  167 us (56%)
  waiting for transfers between devices  86.9 us (29%)
  matrix products  25.1 us (8%)
  between operations  15.4 us (5%)
    all_gather x1, waiting for transfers between devices, body(): lax.all_gather(features, 'blk', axis=0, tiled=True)  86.2 us
    pmax x1, blocking collectives, body(): top = lax.pmax(local_top, ('blk', 'cls'))  74.8 us
    psum x1, blocking collectives, body(): lax.psum(jnp.sum(jnp.exp(logits - top[:, None]), axis=1), ('blk', 'cls'))  73.3 us
    unnamed x1, blocking collectives  18.9 us
    dot_general x1, matrix products, gradient_term(): lax.dot_general(delta, rows, (((0,), (0,)), ((), ())), preferred_element_...  14.6 us
    dot_general x1, matrix products, scores(): lax.dot_general(rows, weight, (((1,), (1,)), ((), ())), preferred_element...  10.5 us
  transfers between devices with their start and end apart: 1, of which 1 were waited for; matrix products, arithmetic and copies ran while one was open for 1% of the time, Pallas kernels for 0%

commit v1 on v0

v1 whole, which is shorter than its diff:
```python
import functools

import jax
import jax.numpy as jnp
from jax import lax
from jax.experimental import pallas as pl
from jax.experimental.pallas import tpu as pltpu
from jax.sharding import PartitionSpec as P

MESH = pl.DeviceIdType.MESH
X, Y, Z = 4, 4, 8
HALF, QUART, WIDE = 32, 16, 1024
PLANE = 256


def rem(a, b):
    return lax.rem(a, jnp.int32(b))


def div(a, b):
    return lax.div(a, jnp.int32(b))


def coords():
    b = lax.axis_index("blk")
    k = lax.axis_index("cls")
    z, h, c = div(b, 4), rem(div(b, 2), 2), rem(b, 2)
    x, low = div(k, 2), rem(k, 2)
    return b, k, x, 2 * h + low, z, c


def device(x, y, z, c):
    return (z * 4 + div(y, 2) * 2 + c, x * 2 + rem(y, 2))


def lse_of(parts):
    m = parts[0]
    for v in parts[1:]:
        m = jnp.maximum(m, v)
    s = jnp.exp(parts[0] - m)
    for v in parts[1:]:
        s = s + jnp.exp(v - m)
    return m + jnp.log(s)


def gather_kernel(
    off_ref, feat_hbm, lab_ref, other_ref, w_hbm,
    f_ref, d_ref, own_ref,
    w_ref, lt_ref, msg, got_p, msg_z, got_z, msg_c, got_c,
    wsem, lsem, isem, isend, zsem, zsend, xysem, xysend, dsem, dsend, csem, csend,
    psem, psend, z2sem, z2send, c2sem, c2send,
):
    b, k, x, y, z, c = coords()
    par, low, high = rem(x, 2), rem(y, 2), div(y, 2)
    up, down = rem(z + 1, Z), rem(z + Z - 1, Z)
    xr, xl = rem(x + 1, X), rem(x + X - 1, X)
    yr, yl = rem(y + 1, Y), rem(y + Y - 1, Y)
    sibling = device(x, y, z, 1 - c)

    plane_peers = [
        device(rem(x + i // 4, X), rem(y + i % 4, Y), z, c) for i in range(1, 16)
    ]
    z_peers = [device(x, y, rem(z + i, Z), c) for i in range(1, 8)]
    cross = device(x, 3 - y, z, 1 - c)

    w_copy = pltpu.make_async_copy(w_hbm, w_ref, wsem)
    w_copy.start()

    barrier = pltpu.get_barrier_semaphore()
    for peer in plane_peers + z_peers + [sibling, cross]:
        pl.semaphore_signal(barrier, inc=1, device_id=peer, device_id_type=MESH)
    pl.semaphore_wait(barrier, 24)

    def rows(start, size):
        return pl.ds(pl.multiple_of(start, 16), size)

    def unit(zz, hh, cc, half):
        return zz * PLANE + hh * 128 + cc * 64 + half * HALF

    def send(src, dst, ssem, rsem, dev):
        return pltpu.make_async_remote_copy(
            src_ref=src, dst_ref=dst, send_sem=ssem, recv_sem=rsem,
            device_id=dev, device_id_type=MESH,
        )

    first = unit(z, low, par, c)
    holder = par == c
    mine = low == high

    def first_to(i, dev):
        start = unit(z, high, c, i)
        return send(
            feat_hbm.at[pl.ds(i * HALF, HALF), :], f_ref.at[rows(start, HALF), :],
            isend.at[i], isem, dev,
        )

    def first_local(i):
        start = unit(z, high, c, i)
        return pltpu.make_async_copy(
            feat_hbm.at[pl.ds(i * HALF, HALF), :], f_ref.at[rows(start, HALF), :], lsem
        )

    for i in range(2):
        @pl.when(jnp.logical_and(holder, mine))
        def _():
            @pl.when(c == i)
            def _():
                first_local(i).start()

            @pl.when(c != i)
            def _():
                first_to(i, sibling).start()

        @pl.when(jnp.logical_and(holder, jnp.logical_not(mine)))
        def _():
            first_to(i, device(x, 3 - y, z, jnp.int32(i))).start()

    for i in range(2):
        @pl.when(jnp.logical_and(jnp.logical_and(holder, mine), c == i))
        def _():
            first_local(i).wait()

    @pl.when(jnp.logical_not(jnp.logical_and(holder, mine)))
    def _():
        at = f_ref.at[rows(first, HALF), :]
        send(at, at, isend.at[0], isem, sibling).wait_recv()

    w_copy.wait()

    def plane_of(j):
        step = div(j + 1, 2)
        return rem(jnp.where(rem(j, 2) == 1, z - step, z + step) + Z, Z)

    def piece(start, size):
        return f_ref.at[rows(start, size), :]

    def to_z(zz, start, size, slot, dev):
        at = piece(start, size)
        return send(at, at, zsend.at[slot], zsem.at[zz], dev)

    def to_xy(zz, start, i):
        dev = [
            device(xr, y, z, c), device(xl, y, z, c), device(x, yr, z, c), device(x, yl, z, c),
        ][i]
        at = piece(start + (i % 2) * QUART, QUART)
        return send(at, at, xysend.at[i, zz], xysem.at[i, zz], dev)

    def to_diag(zz, i):
        if i < 2:
            dev = device(x, yr if i == 0 else yl, z, c)
            start, cols = unit(zz, low, 1 - par, c), 0
        else:
            dev = device(xr if i == 2 else xl, y, z, c)
            start, cols = unit(zz, 1 - low, par, c), WIDE
        at = f_ref.at[rows(start + (i % 2) * QUART, QUART), pl.ds(cols, WIDE)]
        return send(at, at, dsend.at[i, zz], dsem.at[zz], dev)

    def to_sibling(zz, i):
        hh = low if i in (0, 1) else 1 - low
        cc = par if i in (0, 2) else 1 - par
        at = piece(unit(zz, hh, cc, c), HALF)
        return send(at, at, csend.at[i, zz], csem.at[zz], sibling)

    up_dev, down_dev = device(x, y, up, c), device(x, y, down, c)

    def step(n, carry):
        @pl.when(n < 8)
        def _():
            j = n
            zz = plane_of(j)
            start = unit(zz, low, par, c)

            @pl.when(j > 0)
            def _():
                to_z(zz, start, HALF, 0, up_dev).wait_recv()

            odd = rem(j, 2) == 1

            @pl.when(jnp.logical_or(j == 0, jnp.logical_and(odd, j < 5)))
            def _():
                to_z(zz, start, HALF, div(j + 1, 2), up_dev).start()

            @pl.when(jnp.logical_and(jnp.logical_not(odd), j < 5))
            def _():
                to_z(zz, start, HALF, 4 + div(j, 2), down_dev).start()

            @pl.when(j == 5)
            def _():
                to_z(zz, start, QUART, 3, up_dev).start()

            @pl.when(j == 6)
            def _():
                to_z(zz, start + QUART, QUART, 7, down_dev).start()

            for i in range(4):
                to_xy(zz, start, i).start()
            to_sibling(zz, 0).start()

        @pl.when(jnp.logical_and(n >= 1, n < 9))
        def _():
            zz = plane_of(n - 1)
            for i in range(4):
                src = unit(zz, low, 1 - par, c) if i < 2 else unit(zz, 1 - low, par, c)
                to_xy(zz, src, i).wait_recv()
            for i in range(4):
                to_diag(zz, i).start()
            to_sibling(zz, 1).start()
            to_sibling(zz, 2).start()

        @pl.when(jnp.logical_and(n >= 2, n < 10))
        def _():
            zz = plane_of(n - 2)
            at = piece(unit(zz, 1 - low, 1 - par, c), HALF)
            send(at, at, dsend.at[0, zz], dsem.at[zz], sibling).wait_recv()
            to_sibling(zz, 3).start()

        @pl.when(n >= 3)
        def _():
            zz = plane_of(n - 3)
            at = piece(zz * PLANE, 128)
            send(at, at, csend.at[0, zz], csem.at[zz], sibling).wait_recv()
            cols = pl.ds(pl.multiple_of(zz * PLANE, PLANE), PLANE)
            lt = lax.dot_general(
                w_ref[...], f_ref[cols, :], (((1,), (1,)), ((), ())),
                preferred_element_type=jnp.float32,
            )
            lt_ref[:, cols] = lt
            m = jnp.max(lt, axis=0, keepdims=True)
            s = jnp.sum(jnp.exp(lt - m), axis=0, keepdims=True)
            msg[0:1, cols] = m + jnp.log(s)

        return carry

    lax.fori_loop(0, 11, step, 0)

    lane = lax.broadcasted_iota(jnp.int32, (1, 2048), 1)
    msg[1:2, :] = jnp.where(div(lane, 64) == b, lab_ref[...].astype(jnp.float32), -1.0)

    def exchange(src, dst, ssems, rsems, peers):
        copies = [
            send(src, dst.at[i], ssems.at[i], rsems.at[i], peer) for i, peer in enumerate(peers)
        ]
        for copy in copies:
            copy.start()
        for copy in copies:
            copy.wait()

    def merged(src, dst, n):
        lse = lse_of([src[0:1, :]] + [dst[i, 0:1, :] for i in range(n)])
        lab = src[1:2, :]
        for i in range(n):
            lab = jnp.maximum(lab, dst[i, 1:2, :])
        return lse, lab

    exchange(msg, got_p, psend, psem, plane_peers)
    lse, lab = merged(msg, got_p, 15)
    msg_z[0:1, :] = lse
    msg_z[1:2, :] = lab
    exchange(msg_z, got_z, z2send, z2sem, z_peers)
    lse, lab = merged(msg_z, got_z, 7)
    msg_c[0:1, :] = lse
    msg_c[1:2, :] = lab
    exchange(msg_c, got_c, c2send, c2sem, [sibling])
    slab, lab = merged(msg_c, got_c, 1)
    other = other_ref[...]
    high_lse = jnp.maximum(slab, other)
    lse = high_lse + jnp.log(jnp.exp(slab - high_lse) + jnp.exp(other - high_lse))
    msg[0:1, :] = lse
    msg[1:2, :] = lab
    at = msg[0:1, pl.ds(pl.multiple_of(div(b, 2) * 128, 128), 128)]
    own_ref[...] = jnp.where(rem(b, 2) == 1, at[:, 64:], at[:, :64])

    base = off_ref[0] + (b * 8 + k) * 512

    def delta(n, carry):
        cols = pl.ds(pl.multiple_of(n * PLANE, PLANE), PLANE)
        local = msg[1:2, cols].astype(jnp.int32) - base
        hot = lax.broadcasted_iota(jnp.int32, (512, PLANE), 0) == local
        p = jnp.exp(lt_ref[:, cols] - msg[0:1, cols])
        d_ref[:, cols] = (p - jnp.where(hot, 1.0, 0.0)).astype(jnp.bfloat16)
        return carry

    lax.fori_loop(0, 8, delta, 0)

    for i in range(2):
        @pl.when(jnp.logical_and(holder, jnp.logical_not(jnp.logical_and(mine, c == i))))
        def _():
            first_to(i, sibling).wait_send()
    for slot in range(8):
        to_z(z, first, QUART if slot in (3, 7) else HALF, slot, up_dev).wait_send()

    def drain(zz, carry):
        for i in range(4):
            to_xy(zz, first, i).wait_send()
            to_diag(zz, i).wait_send()
            to_sibling(zz, i).wait_send()
        return carry

    lax.fori_loop(0, 8, drain, 0)


def gather(offset, features, labels, other, weight):
    dma = pltpu.SemaphoreType.DMA
    any_spec = pl.BlockSpec(memory_space=pl.ANY)
    vmem = pl.BlockSpec(memory_space=pltpu.VMEM)
    return pl.pallas_call(
        gather_kernel,
        out_shape=(
            jax.ShapeDtypeStruct((2048, 2048), jnp.bfloat16),
            jax.ShapeDtypeStruct((512, 2048), jnp.bfloat16),
            jax.ShapeDtypeStruct((1, 64), jnp.float32),
        ),
        in_specs=[pl.BlockSpec(memory_space=pltpu.SMEM), any_spec, vmem, vmem, any_spec],
        out_specs=(vmem, vmem, vmem),
        scratch_shapes=[
            pltpu.VMEM((512, 2048), jnp.bfloat16),
            pltpu.VMEM((512, 2048), jnp.float32),
            pltpu.VMEM((2, 2048), jnp.float32),
            pltpu.VMEM((15, 2, 2048), jnp.float32),
            pltpu.VMEM((2, 2048), jnp.float32),
            pltpu.VMEM((7, 2, 2048), jnp.float32),
            pltpu.VMEM((2, 2048), jnp.float32),
            pltpu.VMEM((1, 2, 2048), jnp.float32),
            dma, dma, dma, dma((2,)), dma((8,)), dma((8,)),
            dma((4, 8)), dma((4, 8)), dma((8,)), dma((4, 8)), dma((8,)), dma((4, 8)),
            dma((15,)), dma((15,)), dma((7,)), dma((7,)), dma((1,)), dma((1,)),
        ],
        compiler_params=pltpu.CompilerParams(
            collective_id=0, has_side_effects=True, vmem_limit_bytes=40 << 20
        ),
    )(offset, features, labels, other, weight)


def update_kernel(d_ref, f_ref, w_ref, a_ref, nw_ref, na_ref):
    grad = jnp.dot(d_ref[...], f_ref[...], preferred_element_type=jnp.float32)
    acc = a_ref[...] + grad * grad
    na_ref[...] = acc
    step = 0.05 * grad / (jnp.sqrt(acc) + 1e-10)
    nw_ref[...] = (w_ref[...].astype(jnp.float32) - step).astype(jnp.bfloat16)


def update(delta, rows, weight, accum, tile=256):
    col = lambda i: (0, i)
    return pl.pallas_call(
        update_kernel,
        grid=(2048 // tile,),
        out_shape=(
            jax.ShapeDtypeStruct((512, 2048), jnp.bfloat16),
            jax.ShapeDtypeStruct((512, 2048), jnp.float32),
        ),
        in_specs=[
            pl.BlockSpec((512, 2048), lambda i: (0, 0)),
            pl.BlockSpec((2048, tile), col),
            pl.BlockSpec((512, tile), col),
            pl.BlockSpec((512, tile), col),
        ],
        out_specs=(pl.BlockSpec((512, tile), col), pl.BlockSpec((512, tile), col)),
        compiler_params=pltpu.CompilerParams(vmem_limit_bytes=24 << 20),
    )(delta, rows, weight, accum)


def body(features, labels, offset, other_lse, weight, accum):
    tiled = jnp.tile(labels, 32).reshape(1, 2048)
    rows, delta, own = gather(offset, features, tiled, other_lse.reshape(1, 2048), weight)
    new_weight, new_accum = update(delta, rows, weight, accum)
    return (new_weight, new_accum, own.reshape(64))


def solution(mesh):
    in_specs = (
        P("blk", None),
        P("blk"),
        P(),
        P(),
        P(("blk", "cls"), None),
        P(("blk", "cls"), None),
    )
    out_specs = (P(("blk", "cls"), None), P(("blk", "cls"), None), P("blk"))
    return jax.shard_map(body, mesh=mesh, in_specs=in_specs, out_specs=out_specs, check_vma=False)
```

time: 300 us -> 82.8 us (0.28)
  blocking collectives: 167 us -> 0 us
  waiting for transfers between devices: 86.9 us -> 0 us
  Pallas kernels: 0 us -> 74.6 us
  matrix products: 25.1 us -> 0 us
  between operations: 15.4 us -> 1.3 us
  local copies, waits for them, and re-layouts: 2.74 us -> 6.67 us
    all_gather x1 -> x0, waiting for transfers between devices: 86.2 us -> none  [body(): lax.all_gather(features, 'blk', axis=0, tiled=True)]
    pmax x1 -> x0, blocking collectives: 74.8 us -> none  [body(): top = lax.pmax(local_top, ('blk', 'cls'))]
    pallas_call x0 -> x2, Pallas kernels: none -> 74.6 us  [the longest x1 64.8 us: gather(): pl.pallas_call(gather_kernel, out_shape=(jax.ShapeDtypeStruct((2048, 2048...]
    psum x1 -> x0, blocking collectives: 73.3 us -> none  [body(): lax.psum(jnp.sum(jnp.exp(logits - top[:, None]), axis=1), ('blk', 'cls'))]
    dot_general x2 -> x0, matrix products: 25.1 us -> none  [the longest x1 14.6 us: gradient_term(): lax.dot_general(delta, rows, (((0,), (0,)), ((), ())), preferred_element_...]
    unnamed x1 -> x0, blocking collectives: 18.9 us -> none
    unnamed x7 -> x9, local copies, waits for them, and re-layouts: 2.15 us -> 5.93 us
  transfers between devices with their start and end apart: 1 -> 0, of which waited for: 1 -> 0; matrix products, arithmetic and copies ran while one was open for 1% -> 0% of each run, Pallas kernels for 0% -> 0%
where the time goes in v1:
time: 82.8 us; the launch traced here: 82.5 us
  Pallas kernels  74.6 us (90%)
  local copies, waits for them, and re-layouts  6.67 us (8%)
  between operations  1.3 us (2%)
    pallas_call x1, Pallas kernels, gather(): pl.pallas_call(gather_kernel, out_shape=(jax.ShapeDtypeStruct((2048, 2048...  64.8 us
    pallas_call x1, Pallas kernels, update(): pl.pallas_call(update_kernel, grid=(2048 // tile,), out_shape=(jax.ShapeD...  9.78 us
    unnamed x9, local copies, waits for them, and re-layouts  5.93 us

profile of v1, /device:TPU:1, one launch (start us, length us, event | category | flops | bytes accessed | tf_op | source)
XLA Modules:
  0.0 82.5 jit_solution(4597277276869000886)
XLA Ops:
  1.3 0.7 tile.2
  1.9 0.1 reshape_tile.3.lab_ref
  2.0 0.0 copy-start
  2.0 1.6 %copy-done = bf16[512,2048]{1,0:T(8,128)(2,1)S(1)} copy-done((bf16[512,2048]{1,0:T(8,128)(2,1)S(1)}, bf16[512,2048]{1,0:T(8,128)(2,1)}, u32[]{:S(2)}) %copy-start) | copy-done | bytes 2097176
  3.6 0.0 copy-start.2
  3.6 0.9 %copy-done.2 = bf16[64,2048]{1,0:T(8,128)(2,1)S(1)} copy-done((bf16[64,2048]{1,0:T(8,128)(2,1)S(1)}, bf16[64,2048]{1,0:T(8,128)(2,1)}, u32[]{:S(2)}) %copy-start.2) | copy-done | bytes 262168
  4.6 0.0 copy-start.3
  4.6 0.7 copy-done.3
  5.3 64.8 %shard_map.85 = (bf16[2048,2048]{1,0:T(8,128)(2,1)S(1)}, bf16[512,2048]{1,0:T(8,128)(2,1)S(1)}, f32[1,64]{1,0:T(1,128)S(1)}) custom-call(s32[1]{0:T(128)S(6)} %copy.10.off_ref, bf16[64,2048]{1,0:T(8,128)(2,1)S(1)} %copy-done.2, s32[1,2048]{1,0:T(1,128)S(1)} %reshape_tile.3.lab_ref, f32[1,2048]{1,0:T(1,128)S(1)} %bitcast.2, bf16[512,2048]{1,0:T(8,128)(2,1)S(1)} %copy-done), custom_call_target="tpu_custom_call" | custom-call | tf_op jit(solution)/shard_map/pallas_call | solution.py:306
  70.0 0.0 copy-start.1
  70.1 2.2 %copy-done.1 = f32[512,2048]{1,0:T(8,128)S(1)} copy-done((f32[512,2048]{1,0:T(8,128)S(1)}, f32[512,2048]{1,0:T(8,128)}, u32[]{:S(2)}) %copy-start.1) | copy-done | bytes 4194328
  72.2 9.8 %shard_map.86 = (bf16[512,2048]{1,0:T(8,128)(2,1)}, f32[512,2048]{1,0:T(8,128)}) custom-call(bf16[512,2048]{1,0:T(8,128)(2,1)S(1)} %get-tuple-element.8.d_ref, bf16[2048,2048]{1,0:T(8,128)(2,1)S(1)} %get-tuple-element.9.f_ref, bf16[512,2048]{1,0:T(8,128)(2,1)S(1)} %copy-done, f32[512,2048]{1,0:T(8,128)S(1)} %copy-done.1), custom_call_target="tpu_custom_call" | custom-call | tf_op jit(solution)/shard_map/pallas_call | solution.py:344
  82.0 0.5 copy.11
Async XLA Ops:
  2.0 1.6 %copy-start = (bf16[512,2048]{1,0:T(8,128)(2,1)S(1)}, bf16[512,2048]{1,0:T(8,128)(2,1)}, u32[]{:S(2)}) copy-start(bf16[512,2048]{1,0:T(8,128)(2,1)} %w_ref.1) | copy-start | bytes 6291460
  3.6 0.9 %copy-start.2 = (bf16[64,2048]{1,0:T(8,128)(2,1)S(1)}, bf16[64,2048]{1,0:T(8,128)(2,1)}, u32[]{:S(2)}) copy-start(bf16[64,2048]{1,0:T(8,128)(2,1)} %feat_hbm.1) | copy-start | bytes 786436
  4.6 0.7 copy-start.3
  70.0 2.2 %copy-start.1 = (f32[512,2048]{1,0:T(8,128)S(1)}, f32[512,2048]{1,0:T(8,128)}, u32[]{:S(2)}) copy-start(f32[512,2048]{1,0:T(8,128)} %a_ref.1) | copy-start | bytes 12582916

commit v2 on v0

v2 whole, which is shorter than its diff:
```python
import jax
import jax.numpy as jnp
from jax import lax
from jax.experimental import pallas as pl
from jax.experimental.pallas import tpu as pltpu
from jax.sharding import PartitionSpec as P

MESH = pl.DeviceIdType.MESH
X, Y, Z = 4, 4, 8
HALF, QUART, WIDE = 32, 16, 1024
PLANE = 256
OFFSET = (0, -1, 1, -2, 2, -3, 3, 4)
SLOT = {o % Z: j for j, o in enumerate(OFFSET)}
LANES = 128


def rem(a, b):
    return lax.rem(a, jnp.int32(b))


def div(a, b):
    return lax.div(a, jnp.int32(b))


def coords():
    b = lax.axis_index("blk")
    k = lax.axis_index("cls")
    z, h, c = div(b, 4), rem(div(b, 2), 2), rem(b, 2)
    x, low = div(k, 2), rem(k, 2)
    return b, k, x, 2 * h + low, z, c


def device(x, y, z, c):
    return (z * 4 + div(y, 2) * 2 + c, x * 2 + rem(y, 2))


def lse_of(parts):
    m = parts[0]
    for v in parts[1:]:
        m = jnp.maximum(m, v)
    s = jnp.exp(parts[0] - m)
    for v in parts[1:]:
        s = s + jnp.exp(v - m)
    return m + jnp.log(s)


def max_of(parts):
    m = parts[0]
    for v in parts[1:]:
        m = jnp.maximum(m, v)
    return m


def gather_kernel(
    off_ref, feat_hbm, lab_hbm, other_hbm, w_hbm, a_hbm,
    f_ref, d_ref, w_ref, a_ref, own_ref,
    lab_ref, other_ref, lt_ref, msg, got_p, msg_z, got_z, msg_c, got_c,
    wsem, asem, osem, lsem, isem, isend, zsem, zsend, xysem, xysend, dsem, dsend, csem, csend,
    psem, psend, z2sem, z2send, c2sem, c2send,
):
    b, k, x, y, z, c = coords()
    par, low, high = rem(x, 2), rem(y, 2), div(y, 2)
    up, down = rem(z + 1, Z), rem(z + Z - 1, Z)
    xr, xl = rem(x + 1, X), rem(x + X - 1, X)
    yr, yl = rem(y + 1, Y), rem(y + Y - 1, Y)
    sibling = device(x, y, z, 1 - c)
    up_dev, down_dev = device(x, y, up, c), device(x, y, down, c)
    xr_dev, xl_dev = device(xr, y, z, c), device(xl, y, z, c)
    yr_dev, yl_dev = device(x, yr, z, c), device(x, yl, z, c)
    cross = device(x, 3 - y, z, 1 - c)

    plane_peers = [
        device(rem(x + i // 4, X), rem(y + i % 4, Y), z, c) for i in range(1, 16)
    ]
    z_peers = [device(x, y, rem(z + i, Z), c) for i in range(1, 8)]

    w_copy = pltpu.make_async_copy(w_hbm, w_ref, wsem)
    w_copy.start()
    a_copy = pltpu.make_async_copy(a_hbm, a_ref, asem)
    a_copy.start()
    lab_copy = pltpu.make_async_copy(lab_hbm, lab_ref, osem.at[0])
    lab_copy.start()
    other_copy = pltpu.make_async_copy(other_hbm, other_ref, osem.at[1])
    other_copy.start()

    barrier = pltpu.get_barrier_semaphore()
    near = [xr_dev, xl_dev, yr_dev, yl_dev, up_dev, down_dev, sibling, cross]
    for peer in near:
        pl.semaphore_signal(barrier, inc=1, device_id=peer, device_id_type=MESH)
    pl.semaphore_wait(barrier, len(near))

    def rows(start, size):
        return pl.ds(pl.multiple_of(start, 16), size)

    def unit(hh, cc):
        return hh * 128 + cc * 64 + c * HALF

    mine_at = unit(low, par)
    x_at = unit(low, 1 - par)
    y_at = unit(1 - low, par)
    diag_at = unit(1 - low, 1 - par)

    def send(src, dst, ssem, rsem, dev):
        return pltpu.make_async_remote_copy(
            src_ref=src, dst_ref=dst, send_sem=ssem, recv_sem=rsem,
            device_id=dev, device_id_type=MESH,
        )

    holder = par == c
    mine = low == high

    def first_refs(i, q):
        start = high * 128 + c * 64 + i * HALF + q * QUART
        return (
            feat_hbm.at[pl.ds(i * HALF + q * QUART, QUART), :],
            f_ref.at[0, rows(start, QUART), :],
        )

    def first_to(i, q, dev):
        src, dst = first_refs(i, q)
        return send(src, dst, isend.at[i, q], isem.at[q], dev)

    def first_local(i, q):
        src, dst = first_refs(i, q)
        return pltpu.make_async_copy(src, dst, lsem.at[q])

    local = jnp.logical_and(holder, mine)
    for q in range(2):
        for i in range(2):
            @pl.when(jnp.logical_and(local, c == i))
            def _():
                first_local(i, q).start()

            @pl.when(jnp.logical_and(local, c != i))
            def _():
                first_to(i, q, sibling).start()

            @pl.when(jnp.logical_and(holder, jnp.logical_not(mine)))
            def _():
                first_to(i, q, device(x, 3 - y, z, jnp.int32(i))).start()

    def first_wait(q):
        for i in range(2):
            @pl.when(jnp.logical_and(local, c == i))
            def _():
                first_local(i, q).wait()

        @pl.when(jnp.logical_not(local))
        def _():
            at = f_ref.at[0, rows(mine_at + q * QUART, QUART), :]
            send(at, at, isend.at[0, q], isem.at[q], sibling).wait_recv()

    def piece(slot, start, size):
        return f_ref.at[slot, rows(start, size), :]

    def to_z(slot, dst_slot, q, dev):
        start = mine_at + q * QUART
        return send(
            piece(slot, start, QUART), piece(dst_slot, start, QUART),
            zsend.at[dst_slot, q], zsem.at[dst_slot, q], dev,
        )

    def z_wait(slot, q):
        to_z(slot, slot, q, up_dev).wait_recv()

    def region(s, n, start, size, cols=slice(None)):
        lo = max(2 * s - 1, 0) if isinstance(s, int) else jnp.maximum(2 * s - 1, 0)
        return f_ref.at[pl.ds(lo, n), rows(start, size), cols]

    def to_xy(s, n, i, start):
        at = region(s, n, start + (i % 2) * QUART, QUART)
        dev = (xr_dev, xl_dev, yr_dev, yl_dev)[i]
        return send(at, at, xysend.at[i, s], xysem.at[i, s], dev)

    def to_diag(s, n, i):
        start, cols = (x_at, 0) if i < 2 else (y_at, WIDE)
        at = region(s, n, start + (i % 2) * QUART, QUART, pl.ds(cols, WIDE))
        dev = (yr_dev, yl_dev, xr_dev, xl_dev)[i]
        return send(at, at, dsend.at[i, s], dsem.at[i, s], dev)

    def diag_wait(s, n, i):
        cols = 0 if i < 2 else WIDE
        at = region(s, n, diag_at + (i % 2) * QUART, QUART, pl.ds(cols, WIDE))
        send(at, at, dsend.at[i, s], dsem.at[i, s], sibling).wait_recv()

    def to_sibling(s, n, i):
        at = region(s, n, (mine_at, x_at, y_at, diag_at)[i], HALF)
        return send(at, at, csend.at[i, s], csem.at[i, s], sibling)

    def each(s, go):
        pair = jnp.logical_and(s > 0, s < 4)
        pl.when(pair)(lambda: go(s, 2))
        pl.when(jnp.logical_not(pair))(lambda: go(s, 1))

    def step(n, carry):
        @pl.when(n < 5)
        def _():
            for q in range(2):
                @pl.when(n == 0)
                def _():
                    first_wait(q)
                    to_z(0, 1, q, up_dev).start()
                    to_z(0, 2, q, down_dev).start()

                @pl.when(jnp.logical_and(n > 0, n < 3))
                def _():
                    z_wait(2 * n - 1, q)
                    to_z(2 * n - 1, 2 * n + 1, q, up_dev).start()
                    z_wait(2 * n, q)
                    to_z(2 * n, 2 * n + 2, q, down_dev).start()

                @pl.when(n == 3)
                def _():
                    z_wait(5, q)
                    z_wait(6, q)
                    if q == 0:
                        to_z(5, 7, 0, up_dev).start()
                    else:
                        to_z(6, 7, 1, down_dev).start()

                @pl.when(n == 4)
                def _():
                    z_wait(7, q)

            def go(s, m):
                for i in range(4):
                    to_xy(s, m, i, mine_at).start()
                to_sibling(s, m, 0).start()

            each(n, go)

        @pl.when(jnp.logical_and(n >= 1, n < 6))
        def _():
            def go(s, m):
                for i in range(4):
                    to_xy(s, m, i, x_at if i < 2 else y_at).wait_recv()
                    to_diag(s, m, i).start()
                to_sibling(s, m, 1).start()
                to_sibling(s, m, 2).start()

            each(n - 1, go)

        @pl.when(jnp.logical_and(n >= 2, n < 7))
        def _():
            def go(s, m):
                for i in range(4):
                    diag_wait(s, m, i)
                to_sibling(s, m, 3).start()

            each(n - 2, go)

        @pl.when(n == 3)
        def _():
            w_copy.wait()

        @pl.when(n >= 3)
        def _():
            s = n - 3

            def go(s, m):
                for i in range(4):
                    to_sibling(s, m, i).wait_recv()

            each(s, go)

            def scores(slot, carry):
                lt = lax.dot_general(
                    w_ref[...], f_ref[slot], (((1,), (1,)), ((), ())),
                    preferred_element_type=jnp.float32,
                )
                lt_ref[slot] = lt
                m = jnp.max(lt, axis=0, keepdims=True)
                v = m + jnp.log(jnp.sum(jnp.exp(lt - m), axis=0, keepdims=True))
                msg[pl.ds(2 * slot, 1), :] = v[:, :LANES]
                msg[pl.ds(2 * slot + 1, 1), :] = v[:, LANES:]
                return carry

            lo = jnp.maximum(2 * s - 1, 0)
            hi = jnp.where(s < 4, 2 * s + 1, 8)
            lax.fori_loop(lo, hi, scores, 0)

        return carry

    lab_copy.wait()
    other_copy.wait()
    lane = lax.broadcasted_iota(jnp.int32, (16, LANES), 1)
    line = lax.broadcasted_iota(jnp.int32, (16, LANES), 0)
    twice = jnp.concatenate([lab_ref[...], lab_ref[...]], axis=1)
    own_spot = jnp.logical_and(line == high, div(lane, 64) == c)
    msg[16:32, :] = jnp.where(own_spot, twice.astype(jnp.float32), -1.0)

    lax.fori_loop(0, 8, step, 0)

    def exchange(src, dst, ssems, rsems, peers):
        copies = [
            send(src, dst.at[i], ssems.at[i], rsems.at[i], peer) for i, peer in enumerate(peers)
        ]
        for copy in copies:
            copy.start()
        for copy in copies:
            copy.wait()

    exchange(msg, got_p, psend, psem, plane_peers)
    msg_z[0:16, :] = lse_of([msg[0:16, :]] + [got_p[i, 0:16, :] for i in range(15)])
    msg_z[16:32, :] = max_of([msg[16:32, :]] + [got_p[i, 16:32, :] for i in range(15)])
    exchange(msg_z, got_z, z2send, z2sem, z_peers)
    for j, o in enumerate(OFFSET):
        for base, merge in ((0, lse_of), (16, max_of)):
            parts = [msg_z[base + 2 * j : base + 2 * j + 2, :]]
            for i in range(7):
                at = base + 2 * SLOT[(o + i + 1) % Z]
                parts.append(got_z[i, at : at + 2, :])
            msg_c[base + 2 * j : base + 2 * j + 2, :] = merge(parts)
    exchange(msg_c, got_c, c2send, c2sem, [sibling])
    slab = lse_of([msg_c[0:16, :], got_c[0, 0:16, :]])
    msg[16:32, :] = jnp.maximum(msg_c[16:32, :], got_c[0, 16:32, :])
    other = jnp.concatenate(
        [other_ref[pl.ds(2 * rem(z + o + Z, Z), 2), :] for o in OFFSET], axis=0
    )
    top = jnp.maximum(slab, other)
    msg[0:16, :] = top + jnp.log(jnp.exp(slab - top) + jnp.exp(other - top))
    at = msg[pl.ds(high, 1), :]
    own_ref[...] = jnp.where(c == 1, at[:, 64:], at[:, :64])

    base = off_ref[0] + (b * 8 + k) * 512

    def delta(slot, carry):
        def line_of(at):
            return jnp.concatenate([msg[pl.ds(at, 1), :], msg[pl.ds(at + 1, 1), :]], axis=1)

        lse, lab = line_of(2 * slot), line_of(16 + 2 * slot)
        hot = lax.broadcasted_iota(jnp.int32, (512, PLANE), 0) == lab.astype(jnp.int32) - base
        p = jnp.exp(lt_ref[slot] - lse) - jnp.where(hot, 1.0, 0.0)
        d_ref[:, pl.ds(pl.multiple_of(slot * PLANE, PLANE), PLANE)] = p.astype(jnp.bfloat16)
        return carry

    lax.fori_loop(0, 8, delta, 0)
    a_copy.wait()

    for q in range(2):
        for i in range(2):
            @pl.when(jnp.logical_and(holder, jnp.logical_not(jnp.logical_and(mine, c == i))))
            def _():
                first_to(i, q, sibling).wait_send()
        for slot in range(1, 7):
            to_z(slot, slot, q, up_dev).wait_send()
        to_z(7, 7, q, up_dev).wait_send()
    for s in range(5):
        m = 2 if 0 < s < 4 else 1
        for i in range(4):
            to_xy(s, m, i, mine_at).wait_send()
            to_diag(s, m, i).wait_send()
            to_sibling(s, m, i).wait_send()


def gather(offset, features, labels, other, weight, accum):
    dma = pltpu.SemaphoreType.DMA
    hbm = pl.BlockSpec(memory_space=pltpu.HBM)
    vmem = pl.BlockSpec(memory_space=pltpu.VMEM)
    f32 = jnp.float32
    return pl.pallas_call(
        gather_kernel,
        out_shape=(
            jax.ShapeDtypeStruct((8, PLANE, 2048), jnp.bfloat16),
            jax.ShapeDtypeStruct((512, 2048), jnp.bfloat16),
            jax.ShapeDtypeStruct((512, 2048), jnp.bfloat16),
            jax.ShapeDtypeStruct((512, 2048), f32),
            jax.ShapeDtypeStruct((1, 64), f32),
        ),
        in_specs=[pl.BlockSpec(memory_space=pltpu.SMEM)] + [hbm] * 5,
        out_specs=(vmem,) * 5,
        scratch_shapes=[
            pltpu.VMEM((1, 64), jnp.int32),
            pltpu.VMEM((16, LANES), f32),
            pltpu.VMEM((8, 512, PLANE), f32),
            pltpu.VMEM((32, LANES), f32),
            pltpu.VMEM((15, 32, LANES), f32),
            pltpu.VMEM((32, LANES), f32),
            pltpu.VMEM((7, 32, LANES), f32),
            pltpu.VMEM((32, LANES), f32),
            pltpu.VMEM((1, 32, LANES), f32),
            dma, dma, dma((2,)), dma((2,)), dma((2,)), dma((2, 2)), dma((8, 2)), dma((8, 2)),
            dma((4, 5)), dma((4, 5)), dma((4, 5)), dma((4, 5)), dma((4, 5)), dma((4, 5)),
            dma((15,)), dma((15,)), dma((7,)), dma((7,)), dma((1,)), dma((1,)),
        ],
        compiler_params=pltpu.CompilerParams(
            collective_id=0, has_side_effects=True, vmem_limit_bytes=16 << 20
        ),
    )(offset, *(pltpu.with_memory_space_constraint(v, pltpu.HBM) for v in (features, labels, other, weight, accum)))


TILE = 256
TILES = 2048 // TILE


def update_kernel(
    d_ref, f_ref, w_ref, a_ref, own_ref, nw_hbm, na_hbm, own_hbm, g_ref, nw_ref, na_ref, sem, osem
):
    own_copy = pltpu.make_async_copy(own_ref, own_hbm, osem)
    own_copy.start()

    def cols(t):
        return pl.ds(pl.multiple_of(t * TILE, TILE), TILE)

    def dot(t):
        g_ref[rem(t, 2)] = jnp.dot(
            d_ref[...], f_ref[:, cols(t)], preferred_element_type=jnp.float32
        )

    def copies(t):
        return (
            pltpu.make_async_copy(nw_ref.at[:, cols(t)], nw_hbm.at[:, cols(t)], sem.at[0, t]),
            pltpu.make_async_copy(na_ref.at[:, cols(t)], na_hbm.at[:, cols(t)], sem.at[1, t]),
        )

    def apply(t):
        grad = g_ref[rem(t, 2)]
        acc = a_ref[:, cols(t)] + grad * grad
        na_ref[:, cols(t)] = acc
        step = 0.05 * grad / (jnp.sqrt(acc) + 1e-10)
        nw_ref[:, cols(t)] = (w_ref[:, cols(t)].astype(jnp.float32) - step).astype(jnp.bfloat16)

    dot(jnp.int32(0))

    def both(t, carry):
        dot(t)
        apply(t - 1)
        for copy in copies(t - 1):
            copy.start()
        return carry

    lax.fori_loop(1, TILES, both, 0)
    apply(jnp.int32(TILES - 1))
    for copy in copies(TILES - 1):
        copy.start()
    for t in range(TILES):
        for copy in copies(t):
            copy.wait()
    own_copy.wait()


def update(delta, rows, weight, accum, own):
    vmem = pl.BlockSpec(memory_space=pltpu.VMEM)
    hbm = pl.BlockSpec(memory_space=pltpu.HBM)
    return pl.pallas_call(
        update_kernel,
        out_shape=(
            jax.ShapeDtypeStruct((512, 2048), jnp.bfloat16),
            jax.ShapeDtypeStruct((512, 2048), jnp.float32),
            jax.ShapeDtypeStruct((1, 64), jnp.float32),
        ),
        in_specs=[vmem] * 5,
        out_specs=(hbm,) * 3,
        scratch_shapes=[
            pltpu.VMEM((2, 512, TILE), jnp.float32),
            pltpu.VMEM((512, 2048), jnp.bfloat16),
            pltpu.VMEM((512, 2048), jnp.float32),
            pltpu.SemaphoreType.DMA((2, TILES)),
            pltpu.SemaphoreType.DMA,
        ],
        compiler_params=pltpu.CompilerParams(vmem_limit_bytes=16 << 20),
    )(delta, rows, weight, accum, own)


def body(features, labels, offset, other_lse, weight, accum):
    rows, delta, w, a, own = gather(
        offset, features, labels.reshape(1, 64), other_lse.reshape(16, LANES), weight, accum
    )
    new_weight, new_accum, own = update(delta, rows.reshape(2048, 2048), w, a, own)
    return (new_weight, new_accum, own.reshape(64))


def solution(mesh):
    in_specs = (
        P("blk", None),
        P("blk"),
        P(),
        P(),
        P(("blk", "cls"), None),
        P(("blk", "cls"), None),
    )
    out_specs = (P(("blk", "cls"), None), P(("blk", "cls"), None), P("blk"))
    return jax.shard_map(body, mesh=mesh, in_specs=in_specs, out_specs=out_specs, check_vma=False)
```

time: 300 us -> 67.9 us (0.23)
  blocking collectives: 167 us -> 0 us
  waiting for transfers between devices: 86.9 us -> 0 us
  Pallas kernels: 0 us -> 66.4 us
  matrix products: 25.1 us -> 0 us
  between operations: 15.4 us -> 1.28 us
    all_gather x1 -> x0, waiting for transfers between devices: 86.2 us -> none  [body(): lax.all_gather(features, 'blk', axis=0, tiled=True)]
    pmax x1 -> x0, blocking collectives: 74.8 us -> none  [body(): top = lax.pmax(local_top, ('blk', 'cls'))]
    psum x1 -> x0, blocking collectives: 73.3 us -> none  [body(): lax.psum(jnp.sum(jnp.exp(logits - top[:, None]), axis=1), ('blk', 'cls'))]
    pallas_call x0 -> x2, Pallas kernels: none -> 66.4 us  [the longest x1 57.4 us: gather(): pl.pallas_call(gather_kernel, out_shape=(jax.ShapeDtypeStruct((8, PLANE,...]
    dot_general x2 -> x0, matrix products: 25.1 us -> none  [the longest x1 14.6 us: gradient_term(): lax.dot_general(delta, rows, (((0,), (0,)), ((), ())), preferred_element_...]
    unnamed x1 -> x0, blocking collectives: 18.9 us -> none
  transfers between devices with their start and end apart: 1 -> 0, of which waited for: 1 -> 0; matrix products, arithmetic and copies ran while one was open for 1% -> 0% of each run, Pallas kernels for 0% -> 0%
where the time goes in v2:
time: 67.9 us; the launch traced here: 67.7 us
  Pallas kernels  66.4 us (98%)
  between operations  1.28 us (2%)
    pallas_call x1, Pallas kernels, gather(): pl.pallas_call(gather_kernel, out_shape=(jax.ShapeDtypeStruct((8, PLANE,...  57.4 us
    pallas_call x1, Pallas kernels, update(): pl.pallas_call(update_kernel, out_shape=(jax.ShapeDtypeStruct((512, 2048)...  9.04 us

profile of v2, /device:TPU:1, one launch (start us, length us, event | category | flops | bytes accessed | tf_op | source)
XLA Modules:
  0.0 67.7 jit_solution(16648525895020005380)
XLA Ops:
  1.3 57.4 %shard_map.85 = (bf16[8,256,2048]{2,1,0:T(8,128)(2,1)S(1)}, bf16[512,2048]{1,0:T(8,128)(2,1)S(1)}, bf16[512,2048]{1,0:T(8,128)(2,1)S(1)}, f32[512,2048]{1,0:T(8,128)S(1)}, f32[1,64]{1,0:T(1,128)S(1)}) custom-call(s32[1]{0:T(128)S(6)} %copy.9.off_ref, bf16[64,2048]{1,0:T(8,128)(2,1)} %feat_hbm.1, s32[1,64]{1,0:T(1,128)} %bitcast.6, f32[16,128]{1,0:T(8,128)} %bitcast.5, ...), custom_call_target="tpu_custom_call" | custom-call | tf_op jit(solution)/shard_map/pallas_call | solution.py:361
  58.7 9.0 %shard_map.86 = (bf16[512,2048]{1,0:T(8,128)(2,1)}, f32[512,2048]{1,0:T(8,128)}, f32[1,64]{1,0:T(1,128)}) custom-call(bf16[512,2048]{1,0:T(8,128)(2,1)S(1)} %get-tuple-element.11.d_ref, bf16[2048,2048]{1,0:T(8,128)(2,1)S(1)} %bitcast.4, bf16[512,2048]{1,0:T(8,128)(2,1)S(1)} %get-tuple-element.13.w_ref, f32[512,2048]{1,0:T(8,128)S(1)} %get-tuple-element.14.a_ref, ...), custom_call_target="tpu_custom_call" | custom-call | tf_op jit(solution)/shard_map/pallas_call | solution.py:445

commit v3 on v2

--- a/solution.py
+++ b/solution.py
@@ -12,6 +12,8 @@
 OFFSET = (0, -1, 1, -2, 2, -3, 3, 4)
 SLOT = {o % Z: j for j, o in enumerate(OFFSET)}
 LANES = 128
+PIECES = 4
+PIECE = HALF // PIECES
 
 
 def rem(a, b):
@@ -54,9 +56,9 @@
 def gather_kernel(
     off_ref, feat_hbm, lab_hbm, other_hbm, w_hbm, a_hbm,
     f_ref, d_ref, w_ref, a_ref, own_ref,
-    lab_ref, other_ref, lt_ref, msg, got_p, msg_z, got_z, msg_c, got_c,
+    lab_ref, other_ref, lt_ref, msg, got_p, msg_z, got_z, msg_c, got_c, lab, lab_p, lab_c, own_f,
     wsem, asem, osem, lsem, isem, isend, zsem, zsend, xysem, xysend, dsem, dsend, csem, csend,
-    psem, psend, z2sem, z2send, c2sem, c2send,
+    psem, psend, z2sem, z2send, c2sem, c2send, lpsem, lpsend, lzsem, lzsend, lcsem, lcsend,
 ):
     b, k, x, y, z, c = coords()
     par, low, high = rem(x, 2), rem(y, 2), div(y, 2)
@@ -68,12 +70,15 @@
     xr_dev, xl_dev = device(xr, y, z, c), device(xl, y, z, c)
     yr_dev, yl_dev = device(x, yr, z, c), device(x, yl, z, c)
     cross = device(x, 3 - y, z, 1 - c)
+    diag_devs = [device(i, j, z, c) for j in (yr, yl) for i in (xr, xl)]
 
     plane_peers = [
         device(rem(x + i // 4, X), rem(y + i % 4, Y), z, c) for i in range(1, 16)
     ]
     z_peers = [device(x, y, rem(z + i, Z), c) for i in range(1, 8)]
 
+    f_copy = pltpu.make_async_copy(feat_hbm, own_f, osem.at[2])
+    f_copy.start()
     w_copy = pltpu.make_async_copy(w_hbm, w_ref, wsem)
     w_copy.start()
     a_copy = pltpu.make_async_copy(a_hbm, a_ref, asem)
@@ -88,9 +93,10 @@
     for peer in near:
         pl.semaphore_signal(barrier, inc=1, device_id=peer, device_id_type=MESH)
     pl.semaphore_wait(barrier, len(near))
+    f_copy.wait()
 
     def rows(start, size):
-        return pl.ds(pl.multiple_of(start, 16), size)
+        return pl.ds(pl.multiple_of(start, 8), size)
 
     def unit(hh, cc):
         return hh * 128 + cc * 64 + c * HALF
@@ -110,10 +116,10 @@
     mine = low == high
 
     def first_refs(i, q):
-        start = high * 128 + c * 64 + i * HALF + q * QUART
+        start = high * 128 + c * 64 + i * HALF + q * PIECE
         return (
-            feat_hbm.at[pl.ds(i * HALF + q * QUART, QUART), :],
-            f_ref.at[0, rows(start, QUART), :],
+            own_f.at[pl.ds(i * HALF + q * PIECE, PIECE), :],
+            f_ref.at[0, rows(start, PIECE), :],
         )
 
     def first_to(i, q, dev):
@@ -125,7 +131,7 @@
         return pltpu.make_async_copy(src, dst, lsem.at[q])
 
     local = jnp.logical_and(holder, mine)
-    for q in range(2):
+    for q in range(PIECES):
         for i in range(2):
             @pl.when(jnp.logical_and(local, c == i))
             def _():
@@ -147,16 +153,16 @@
 
         @pl.when(jnp.logical_not(local))
         def _():
-            at = f_ref.at[0, rows(mine_at + q * QUART, QUART), :]
+            at = f_ref.at[0, rows(mine_at + q * PIECE, PIECE), :]
             send(at, at, isend.at[0, q], isem.at[q], sibling).wait_recv()
 
     def piece(slot, start, size):
         return f_ref.at[slot, rows(start, size), :]
 
     def to_z(slot, dst_slot, q, dev):
-        start = mine_at + q * QUART
+        start = mine_at + q * PIECE
         return send(
-            piece(slot, start, QUART), piece(dst_slot, start, QUART),
+            piece(slot, start, PIECE), piece(dst_slot, start, PIECE),
             zsend.at[dst_slot, q], zsem.at[dst_slot, q], dev,
         )
 
@@ -172,17 +178,17 @@
         dev = (xr_dev, xl_dev, yr_dev, yl_dev)[i]
         return send(at, at, xysend.at[i, s], xysem.at[i, s], dev)
 
-    def to_diag(s, n, i):
+    def to_diag(s, n, i, start):
+        cols = pl.ds(i // 2 * WIDE, WIDE)
+        at = region(s, n, start + (i % 2) * QUART, QUART, cols)
+        return send(at, at, dsend.at[i, s], dsem.at[i, s], diag_devs[i])
+
+    def pass_on(s, n, i):
         start, cols = (x_at, 0) if i < 2 else (y_at, WIDE)
         at = region(s, n, start + (i % 2) * QUART, QUART, pl.ds(cols, WIDE))
         dev = (yr_dev, yl_dev, xr_dev, xl_dev)[i]
         return send(at, at, dsend.at[i, s], dsem.at[i, s], dev)
 
-    def diag_wait(s, n, i):
-        cols = 0 if i < 2 else WIDE
-        at = region(s, n, diag_at + (i % 2) * QUART, QUART, pl.ds(cols, WIDE))
-        send(at, at, dsend.at[i, s], dsem.at[i, s], sibling).wait_recv()
-
     def to_sibling(s, n, i):
         at = region(s, n, (mine_at, x_at, y_at, diag_at)[i], HALF)
         return send(at, at, csend.at[i, s], csem.at[i, s], sibling)
@@ -192,10 +198,23 @@
         pl.when(pair)(lambda: go(s, 2))
         pl.when(jnp.logical_not(pair))(lambda: go(s, 1))
 
+    lab_plane = [
+        send(lab.at[0], lab_p.at[i], lpsend.at[i], lpsem.at[i], peer)
+        for i, peer in enumerate(plane_peers)
+    ]
+    lab_z = [
+        (
+            send(lab.at[0], lab.at[SLOT[(-i - 1) % Z]], lzsend.at[i], lzsem.at[i], peer),
+            send(lab.at[0], lab.at[SLOT[(-i - 1) % Z]], lzsend.at[i], lzsem.at[i], peer),
+        )
+        for i, peer in enumerate(z_peers)
+    ]
+    lab_sibling = send(lab, lab_c, lcsend, lcsem, sibling)
+
     def step(n, carry):
         @pl.when(n < 5)
         def _():
-            for q in range(2):
+            for q in range(PIECES):
                 @pl.when(n == 0)
                 def _():
                     first_wait(q)
@@ -213,10 +232,10 @@
                 def _():
                     z_wait(5, q)
                     z_wait(6, q)
-                    if q == 0:
-                        to_z(5, 7, 0, up_dev).start()
+                    if q < PIECES // 2:
+                        to_z(5, 7, q, up_dev).start()
                     else:
-                        to_z(6, 7, 1, down_dev).start()
+                        to_z(6, 7, q, down_dev).start()
 
                 @pl.when(n == 4)
                 def _():
@@ -234,7 +253,7 @@
             def go(s, m):
                 for i in range(4):
                     to_xy(s, m, i, x_at if i < 2 else y_at).wait_recv()
-                    to_diag(s, m, i).start()
+                    pass_on(s, m, i).start()
                 to_sibling(s, m, 1).start()
                 to_sibling(s, m, 2).start()
 
@@ -244,12 +263,17 @@
         def _():
             def go(s, m):
                 for i in range(4):
-                    diag_wait(s, m, i)
+                    to_diag(s, m, i, diag_at).wait_recv()
                 to_sibling(s, m, 3).start()
 
             each(n - 2, go)
 
-        @pl.when(n == 3)
+        @pl.when(n == 5)
+        def _():
+            for copy in lab_plane:
+                copy.start()
+
+        @pl.when(n == 2)
         def _():
             w_copy.wait()
 
@@ -283,11 +307,11 @@
 
     lab_copy.wait()
     other_copy.wait()
-    lane = lax.broadcasted_iota(jnp.int32, (16, LANES), 1)
-    line = lax.broadcasted_iota(jnp.int32, (16, LANES), 0)
+    lane = lax.broadcasted_iota(jnp.int32, (2, LANES), 1)
+    line = lax.broadcasted_iota(jnp.int32, (2, LANES), 0)
     twice = jnp.concatenate([lab_ref[...], lab_ref[...]], axis=1)
     own_spot = jnp.logical_and(line == high, div(lane, 64) == c)
-    msg[16:32, :] = jnp.where(own_spot, twice.astype(jnp.float32), -1.0)
+    lab[0] = jnp.where(own_spot, twice.astype(jnp.float32), -1.0)
 
     lax.fori_loop(0, 8, step, 0)
 
@@ -300,36 +324,42 @@
         for copy in copies:
             copy.wait()
 
+    for copy in lab_plane:
+        copy.wait()
+    lab[0] = max_of([lab[0]] + [lab_p[i] for i in range(15)])
+    for copy, _ in lab_z:
+        copy.start()
     exchange(msg, got_p, psend, psem, plane_peers)
-    msg_z[0:16, :] = lse_of([msg[0:16, :]] + [got_p[i, 0:16, :] for i in range(15)])
-    msg_z[16:32, :] = max_of([msg[16:32, :]] + [got_p[i, 16:32, :] for i in range(15)])
+    msg_z[...] = lse_of([msg[...]] + [got_p[i] for i in range(15)])
     exchange(msg_z, got_z, z2send, z2sem, z_peers)
     for j, o in enumerate(OFFSET):
-        for base, merge in ((0, lse_of), (16, max_of)):
-            parts = [msg_z[base + 2 * j : base + 2 * j + 2, :]]
-            for i in range(7):
-                at = base + 2 * SLOT[(o + i + 1) % Z]
-                parts.append(got_z[i, at : at + 2, :])
-            msg_c[base + 2 * j : base + 2 * j + 2, :] = merge(parts)
+        parts = [msg_z[2 * j : 2 * j + 2, :]]
+        for i in range(7):
+            at = 2 * SLOT[(o + i + 1) % Z]
+            parts.append(got_z[i, at : at + 2, :])
+        msg_c[2 * j : 2 * j + 2, :] = lse_of(parts)
+    for copy, arrived in lab_z:
+        copy.wait_send()
+        arrived.wait_recv()
+    lab_sibling.start()
     exchange(msg_c, got_c, c2send, c2sem, [sibling])
-    slab = lse_of([msg_c[0:16, :], got_c[0, 0:16, :]])
-    msg[16:32, :] = jnp.maximum(msg_c[16:32, :], got_c[0, 16:32, :])
+    slab = lse_of([msg_c[...], got_c[0]])
+    lab_sibling.wait()
     other = jnp.concatenate(
         [other_ref[pl.ds(2 * rem(z + o + Z, Z), 2), :] for o in OFFSET], axis=0
     )
     top = jnp.maximum(slab, other)
-    msg[0:16, :] = top + jnp.log(jnp.exp(slab - top) + jnp.exp(other - top))
+    msg[...] = top + jnp.log(jnp.exp(slab - top) + jnp.exp(other - top))
     at = msg[pl.ds(high, 1), :]
     own_ref[...] = jnp.where(c == 1, at[:, 64:], at[:, :64])
 
     base = off_ref[0] + (b * 8 + k) * 512
 
     def delta(slot, carry):
-        def line_of(at):
-            return jnp.concatenate([msg[pl.ds(at, 1), :], msg[pl.ds(at + 1, 1), :]], axis=1)
-
-        lse, lab = line_of(2 * slot), line_of(16 + 2 * slot)
-        hot = lax.broadcasted_iota(jnp.int32, (512, PLANE), 0) == lab.astype(jnp.int32) - base
+        lse = jnp.concatenate([msg[pl.ds(2 * slot, 1), :], msg[pl.ds(2 * slot + 1, 1), :]], axis=1)
+        ids = jnp.maximum(lab[slot], lab_c[slot])
+        labels = jnp.concatenate([ids[0:1, :], ids[1:2, :]], axis=1).astype(jnp.int32)
+        hot = lax.broadcasted_iota(jnp.int32, (512, PLANE), 0) == labels - base
         p = jnp.exp(lt_ref[slot] - lse) - jnp.where(hot, 1.0, 0.0)
         d_ref[:, pl.ds(pl.multiple_of(slot * PLANE, PLANE), PLANE)] = p.astype(jnp.bfloat16)
         return carry
@@ -337,19 +367,18 @@
     lax.fori_loop(0, 8, delta, 0)
     a_copy.wait()
 
-    for q in range(2):
+    for q in range(PIECES):
         for i in range(2):
             @pl.when(jnp.logical_and(holder, jnp.logical_not(jnp.logical_and(mine, c == i))))
             def _():
                 first_to(i, q, sibling).wait_send()
-        for slot in range(1, 7):
+        for slot in range(1, 8):
             to_z(slot, slot, q, up_dev).wait_send()
-        to_z(7, 7, q, up_dev).wait_send()
     for s in range(5):
         m = 2 if 0 < s < 4 else 1
         for i in range(4):
             to_xy(s, m, i, mine_at).wait_send()
-            to_diag(s, m, i).wait_send()
+            to_diag(s, m, i, mine_at).wait_send()
             to_sibling(s, m, i).wait_send()
 
 
@@ -373,15 +402,21 @@
             pltpu.VMEM((1, 64), jnp.int32),
             pltpu.VMEM((16, LANES), f32),
             pltpu.VMEM((8, 512, PLANE), f32),
-            pltpu.VMEM((32, LANES), f32),
-            pltpu.VMEM((15, 32, LANES), f32),
-            pltpu.VMEM((32, LANES), f32),
-            pltpu.VMEM((7, 32, LANES), f32),
-            pltpu.VMEM((32, LANES), f32),
-            pltpu.VMEM((1, 32, LANES), f32),
-            dma, dma, dma((2,)), dma((2,)), dma((2,)), dma((2, 2)), dma((8, 2)), dma((8, 2)),
+            pltpu.VMEM((16, LANES), f32),
+            pltpu.VMEM((15, 16, LANES), f32),
+            pltpu.VMEM((16, LANES), f32),
+            pltpu.VMEM((7, 16, LANES), f32),
+            pltpu.VMEM((16, LANES), f32),
+            pltpu.VMEM((1, 16, LANES), f32),
+            pltpu.VMEM((8, 2, LANES), f32),
+            pltpu.VMEM((15, 2, LANES), f32),
+            pltpu.VMEM((8, 2, LANES), f32),
+            pltpu.VMEM((64, 2048), jnp.bfloat16),
+            dma, dma, dma((3,)), dma((PIECES,)), dma((PIECES,)), dma((2, PIECES)),
+            dma((8, PIECES)), dma((8, PIECES)),
             dma((4, 5)), dma((4, 5)), dma((4, 5)), dma((4, 5)), dma((4, 5)), dma((4, 5)),
             dma((15,)), dma((15,)), dma((7,)), dma((7,)), dma((1,)), dma((1,)),
+            dma((15,)), dma((15,)), dma((7,)), dma((7,)), dma, dma,
         ],
         compiler_params=pltpu.CompilerParams(
             collective_id=0, has_side_effects=True, vmem_limit_bytes=16 << 20
@@ -389,51 +424,32 @@
     )(offset, *(pltpu.with_memory_space_constraint(v, pltpu.HBM) for v in (features, labels, other, weight, accum)))
 
 
-TILE = 256
-TILES = 2048 // TILE
+TILES = ((0, 1024), (1024, 512), (1536, 512))
 
 
 def update_kernel(
-    d_ref, f_ref, w_ref, a_ref, own_ref, nw_hbm, na_hbm, own_hbm, g_ref, nw_ref, na_ref, sem, osem
+    d_ref, f_ref, w_ref, a_ref, own_ref, nw_hbm, na_hbm, own_hbm, nw_ref, na_ref, sem, osem
 ):
     own_copy = pltpu.make_async_copy(own_ref, own_hbm, osem)
     own_copy.start()
 
-    def cols(t):
-        return pl.ds(pl.multiple_of(t * TILE, TILE), TILE)
-
-    def dot(t):
-        g_ref[rem(t, 2)] = jnp.dot(
-            d_ref[...], f_ref[:, cols(t)], preferred_element_type=jnp.float32
+    def copies(t):
+        cols = pl.ds(*TILES[t])
+        return (
+            pltpu.make_async_copy(nw_ref.at[:, cols], nw_hbm.at[:, cols], sem.at[0, t]),
+            pltpu.make_async_copy(na_ref.at[:, cols], na_hbm.at[:, cols], sem.at[1, t]),
         )
 
-    def copies(t):
-        return (
-            pltpu.make_async_copy(nw_ref.at[:, cols(t)], nw_hbm.at[:, cols(t)], sem.at[0, t]),
-            pltpu.make_async_copy(na_ref.at[:, cols(t)], na_hbm.at[:, cols(t)], sem.at[1, t]),
-        )
-
-    def apply(t):
-        grad = g_ref[rem(t, 2)]
-        acc = a_ref[:, cols(t)] + grad * grad
-        na_ref[:, cols(t)] = acc
-        step = 0.05 * grad / (jnp.sqrt(acc) + 1e-10)
-        nw_ref[:, cols(t)] = (w_ref[:, cols(t)].astype(jnp.float32) - step).astype(jnp.bfloat16)
-
-    dot(jnp.int32(0))
-
-    def both(t, carry):
-        dot(t)
-        apply(t - 1)
-        for copy in copies(t - 1):
+    for t, (at, size) in enumerate(TILES):
+        cols = pl.ds(at, size)
+        grad = jnp.dot(d_ref[...], f_ref[:, cols], preferred_element_type=jnp.float32)
+        acc = a_ref[:, cols] + grad * grad
+        na_ref[:, cols] = acc
+        step = 0.05 * grad / (acc * lax.rsqrt(acc) + 1e-10)
+        nw_ref[:, cols] = (w_ref[:, cols].astype(jnp.float32) - step).astype(jnp.bfloat16)
+        for copy in copies(t):
             copy.start()
-        return carry
-
-    lax.fori_loop(1, TILES, both, 0)
-    apply(jnp.int32(TILES - 1))
-    for copy in copies(TILES - 1):
-        copy.start()
-    for t in range(TILES):
+    for t in range(len(TILES)):
         for copy in copies(t):
             copy.wait()
     own_copy.wait()
@@ -452,10 +468,9 @@
         in_specs=[vmem] * 5,
         out_specs=(hbm,) * 3,
         scratch_shapes=[
-            pltpu.VMEM((2, 512, TILE), jnp.float32),
             pltpu.VMEM((512, 2048), jnp.bfloat16),
             pltpu.VMEM((512, 2048), jnp.float32),
-            pltpu.SemaphoreType.DMA((2, TILES)),
+            pltpu.SemaphoreType.DMA((2, len(TILES))),
             pltpu.SemaphoreType.DMA,
         ],
         compiler_params=pltpu.CompilerParams(vmem_limit_bytes=16 << 20),

time: 67.9 us -> 64 us (0.943)
  Pallas kernels: 66.4 us -> 62.6 us
    pallas_call x1, Pallas kernels: 9.04 us -> 6.67 us  [update(): pl.pallas_call(update_kernel, out_shape=(jax.ShapeDtypeStruct((512, 2048)...]
    pallas_call x1, Pallas kernels: 57.4 us -> 55.9 us  [gather(): pl.pallas_call(gather_kernel, out_shape=(jax.ShapeDtypeStruct((8, PLANE,...]
where the time goes in v3:
time: 64 us; the launch traced here: 63.9 us
  Pallas kernels  62.6 us (98%)
  between operations  1.28 us (2%)
    pallas_call x1, Pallas kernels, gather(): pl.pallas_call(gather_kernel, out_shape=(jax.ShapeDtypeStruct((8, PLANE,...  55.9 us
    pallas_call x1, Pallas kernels, update(): pl.pallas_call(update_kernel, out_shape=(jax.ShapeDtypeStruct((512, 2048)...  6.67 us

profile of v3, /device:TPU:1, one launch (start us, length us, event | category | flops | bytes accessed | tf_op | source)
XLA Modules:
  0.0 63.9 jit_solution(2947598366402289359)
XLA Ops:
  1.3 55.9 %shard_map.85 = (bf16[8,256,2048]{2,1,0:T(8,128)(2,1)S(1)}, bf16[512,2048]{1,0:T(8,128)(2,1)S(1)}, bf16[512,2048]{1,0:T(8,128)(2,1)S(1)}, f32[512,2048]{1,0:T(8,128)S(1)}, f32[1,64]{1,0:T(1,128)S(1)}) custom-call(s32[1]{0:T(128)S(6)} %copy.9.off_ref, bf16[64,2048]{1,0:T(8,128)(2,1)} %feat_hbm.1, s32[1,64]{1,0:T(1,128)} %bitcast.6, f32[16,128]{1,0:T(8,128)} %bitcast.5, ...), custom_call_target="tpu_custom_call" | custom-call | tf_op jit(solution)/shard_map/pallas_call | solution.py:390
  57.2 6.7 %shard_map.86 = (bf16[512,2048]{1,0:T(8,128)(2,1)}, f32[512,2048]{1,0:T(8,128)}, f32[1,64]{1,0:T(1,128)}) custom-call(bf16[512,2048]{1,0:T(8,128)(2,1)S(1)} %get-tuple-element.11.d_ref, bf16[2048,2048]{1,0:T(8,128)(2,1)S(1)} %bitcast.4, bf16[512,2048]{1,0:T(8,128)(2,1)S(1)} %get-tuple-element.13.w_ref, f32[512,2048]{1,0:T(8,128)S(1)} %get-tuple-element.14.a_ref, ...), custom_call_target="tpu_custom_call" | custom-call | tf_op jit(solution)/shard_map/pallas_call | solution.py:461

commit v4 on v3

--- a/solution.py
+++ b/solution.py
@@ -56,9 +56,10 @@
 def gather_kernel(
     off_ref, feat_hbm, lab_hbm, other_hbm, w_hbm, a_hbm,
     f_ref, d_ref, w_ref, a_ref, own_ref,
-    lab_ref, other_ref, lt_ref, msg, got_p, msg_z, got_z, msg_c, got_c, lab, lab_p, lab_c, own_f,
+    lab_ref, other_ref, lt_ref, msg, got_p, msg_z, got_z, fin, lab, lab_p, lab_c, own_f, w_sib, lt_out,
     wsem, asem, osem, lsem, isem, isend, zsem, zsend, xysem, xysend, dsem, dsend, csem, csend,
     psem, psend, z2sem, z2send, c2sem, c2send, lpsem, lpsend, lzsem, lzsend, lcsem, lcsend,
+    wxsem, wxsend, ltsem, ltsend,
 ):
     b, k, x, y, z, c = coords()
     par, low, high = rem(x, 2), rem(y, 2), div(y, 2)
@@ -99,7 +100,7 @@
         return pl.ds(pl.multiple_of(start, 8), size)
 
     def unit(hh, cc):
-        return hh * 128 + cc * 64 + c * HALF
+        return c * 128 + (hh * 2 + cc) * HALF
 
     mine_at = unit(low, par)
     x_at = unit(low, 1 - par)
@@ -116,7 +117,7 @@
     mine = low == high
 
     def first_refs(i, q):
-        start = high * 128 + c * 64 + i * HALF + q * PIECE
+        start = i * 128 + (high * 2 + c) * HALF + q * PIECE
         return (
             own_f.at[pl.ds(i * HALF + q * PIECE, PIECE), :],
             f_ref.at[0, rows(start, PIECE), :],
@@ -189,9 +190,40 @@
         dev = (yr_dev, yl_dev, xr_dev, xl_dev)[i]
         return send(at, at, dsend.at[i, s], dsem.at[i, s], dev)
 
-    def to_sibling(s, n, i):
-        at = region(s, n, (mine_at, x_at, y_at, diag_at)[i], HALF)
-        return send(at, at, csend.at[i, s], csem.at[i, s], sibling)
+    def to_sibling(s, n):
+        at = region(s, n, c * 128, 128)
+        return send(at, at, csend.at[s], csem.at[s], sibling)
+
+    w_sibling = send(w_ref, w_sib, wxsend, wxsem, sibling)
+
+    def lt_sibling(s, n):
+        lo = max(2 * s - 1, 0) if isinstance(s, int) else jnp.maximum(2 * s - 1, 0)
+        return send(
+            lt_out.at[pl.ds(lo, n)], lt_ref.at[c, pl.ds(lo, n)], ltsend.at[s], ltsem.at[s], sibling
+        )
+
+    def scores(s, n):
+        lo = jnp.maximum(2 * s - 1, 0)
+        x = f_ref[pl.ds(lo, n), rows(c * 128, 128), :].reshape(n * 128, 2048)
+        own, other = (
+            lax.dot_general(
+                w[...], x, (((1,), (1,)), ((), ())), preferred_element_type=jnp.float32
+            )
+            for w in (w_ref, w_sib)
+        )
+        m = jnp.maximum(
+            jnp.max(own, axis=0, keepdims=True), jnp.max(other, axis=0, keepdims=True)
+        )
+        total = jnp.sum(jnp.exp(own - m), axis=0, keepdims=True) + jnp.sum(
+            jnp.exp(other - m), axis=0, keepdims=True
+        )
+        v = m + jnp.log(total)
+        for i in range(n):
+            cols = slice(i * 128, (i + 1) * 128)
+            lt_ref[c, lo + i] = own[:, cols]
+            lt_out[lo + i] = other[:, cols]
+            msg[pl.ds(lo + i, 1), :] = v[:, cols]
+        lt_sibling(s, n).start()
 
     def each(s, go):
         pair = jnp.logical_and(s > 0, s < 4)
@@ -212,6 +244,15 @@
     lab_sibling = send(lab, lab_c, lcsend, lcsem, sibling)
 
     def step(n, carry):
+        @pl.when(n == 1)
+        def _():
+            w_copy.wait()
+            w_sibling.start()
+
+        @pl.when(n == 2)
+        def _():
+            w_sibling.wait_recv()
+
         @pl.when(n < 5)
         def _():
             for q in range(PIECES):
@@ -241,12 +282,14 @@
                 def _():
                     z_wait(7, q)
 
-            def go(s, m):
-                for i in range(4):
-                    to_xy(s, m, i, mine_at).start()
-                to_sibling(s, m, 0).start()
-
-            each(n, go)
+                if q % (PIECES // 2) == PIECES // 2 - 1:
+                    side = q // (PIECES // 2)
+
+                    def go(s, m):
+                        for i in (side, 2 + side):
+                            to_xy(s, m, i, mine_at).start()
+
+                    each(n, go)
 
         @pl.when(jnp.logical_and(n >= 1, n < 6))
         def _():
@@ -254,8 +297,6 @@
                 for i in range(4):
                     to_xy(s, m, i, x_at if i < 2 else y_at).wait_recv()
                     pass_on(s, m, i).start()
-                to_sibling(s, m, 1).start()
-                to_sibling(s, m, 2).start()
 
             each(n - 1, go)
 
@@ -264,7 +305,7 @@
             def go(s, m):
                 for i in range(4):
                     to_diag(s, m, i, diag_at).wait_recv()
-                to_sibling(s, m, 3).start()
+                to_sibling(s, m).start()
 
             each(n - 2, go)
 
@@ -273,35 +314,13 @@
             for copy in lab_plane:
                 copy.start()
 
-        @pl.when(n == 2)
-        def _():
-            w_copy.wait()
-
-        @pl.when(n >= 3)
-        def _():
-            s = n - 3
-
-            def go(s, m):
-                for i in range(4):
-                    to_sibling(s, m, i).wait_recv()
-
-            each(s, go)
-
-            def scores(slot, carry):
-                lt = lax.dot_general(
-                    w_ref[...], f_ref[slot], (((1,), (1,)), ((), ())),
-                    preferred_element_type=jnp.float32,
-                )
-                lt_ref[slot] = lt
-                m = jnp.max(lt, axis=0, keepdims=True)
-                v = m + jnp.log(jnp.sum(jnp.exp(lt - m), axis=0, keepdims=True))
-                msg[pl.ds(2 * slot, 1), :] = v[:, :LANES]
-                msg[pl.ds(2 * slot + 1, 1), :] = v[:, LANES:]
+        @pl.when(n >= 4)
+        def _():
+            def ready(s, carry):
+                each(s, scores)
                 return carry
 
-            lo = jnp.maximum(2 * s - 1, 0)
-            hi = jnp.where(s < 4, 2 * s + 1, 8)
-            lax.fori_loop(lo, hi, scores, 0)
+            lax.fori_loop(2 * (n - 4), jnp.minimum(2 * (n - 3), 5), ready, 0)
 
         return carry
 
@@ -309,11 +328,27 @@
     other_copy.wait()
     lane = lax.broadcasted_iota(jnp.int32, (2, LANES), 1)
     line = lax.broadcasted_iota(jnp.int32, (2, LANES), 0)
-    twice = jnp.concatenate([lab_ref[...], lab_ref[...]], axis=1)
-    own_spot = jnp.logical_and(line == high, div(lane, 64) == c)
-    lab[0] = jnp.where(own_spot, twice.astype(jnp.float32), -1.0)
-
-    lax.fori_loop(0, 8, step, 0)
+    spot = high * 2 + c
+    ids = [jnp.concatenate([lab_ref[:, i * 32 : i * 32 + 32]] * 4, axis=1) for i in range(2)]
+    ids = jnp.where(line == 0, ids[0], ids[1]).astype(jnp.float32)
+    lab[0] = jnp.where(div(lane, 32) == spot, ids, -1.0)
+
+    lines = [
+        jnp.concatenate(
+            [other_ref[pl.ds(2 * rem(z + o + Z, Z) + hh, 1), :] for o in OFFSET], axis=0
+        )
+        for hh in range(2)
+    ]
+    halves = [
+        jnp.concatenate(
+            [lines[hh][:, cc * 64 + i * 32 : cc * 64 + i * 32 + 32] for hh in range(2) for cc in range(2)],
+            axis=1,
+        )
+        for i in range(2)
+    ]
+    other_ref[0:8, :] = jnp.where(c == 0, halves[0], halves[1])
+
+    lax.fori_loop(0, 7, step, 0)
 
     def exchange(src, dst, ssems, rsems, peers):
         copies = [
@@ -332,41 +367,51 @@
     exchange(msg, got_p, psend, psem, plane_peers)
     msg_z[...] = lse_of([msg[...]] + [got_p[i] for i in range(15)])
     exchange(msg_z, got_z, z2send, z2sem, z_peers)
+    sums = []
     for j, o in enumerate(OFFSET):
-        parts = [msg_z[2 * j : 2 * j + 2, :]]
+        parts = [msg_z[j : j + 1, :]]
         for i in range(7):
-            at = 2 * SLOT[(o + i + 1) % Z]
-            parts.append(got_z[i, at : at + 2, :])
-        msg_c[2 * j : 2 * j + 2, :] = lse_of(parts)
+            at = SLOT[(o + i + 1) % Z]
+            parts.append(got_z[i, at : at + 1, :])
+        sums.append(parts)
+    slab = lse_of([jnp.concatenate([p[i] for p in sums], axis=0) for i in range(8)])
+    other = other_ref[0:8, :]
+    top = jnp.maximum(slab, other)
+    fin[c] = top + jnp.log(jnp.exp(slab - top) + jnp.exp(other - top))
+    fin_sibling = send(fin.at[c], fin.at[c], c2send, c2sem, sibling)
+    fin_sibling.start()
     for copy, arrived in lab_z:
         copy.wait_send()
         arrived.wait_recv()
     lab_sibling.start()
-    exchange(msg_c, got_c, c2send, c2sem, [sibling])
-    slab = lse_of([msg_c[...], got_c[0]])
+    fin_sibling.wait()
     lab_sibling.wait()
-    other = jnp.concatenate(
-        [other_ref[pl.ds(2 * rem(z + o + Z, Z), 2), :] for o in OFFSET], axis=0
-    )
-    top = jnp.maximum(slab, other)
-    msg[...] = top + jnp.log(jnp.exp(slab - top) + jnp.exp(other - top))
-    at = msg[pl.ds(high, 1), :]
-    own_ref[...] = jnp.where(c == 1, at[:, 64:], at[:, :64])
+    for s in range(5):
+        lt_sibling(s, 2 if 0 < s < 4 else 1).wait()
+
+    def own_part(v):
+        part = v[:, 0:32]
+        for i in range(1, 4):
+            part = jnp.where(spot == i, v[:, i * 32 : i * 32 + 32], part)
+        return part
+
+    own_ref[...] = jnp.concatenate([own_part(fin[i, 0:1, :]) for i in range(2)], axis=1)
 
     base = off_ref[0] + (b * 8 + k) * 512
 
     def delta(slot, carry):
-        lse = jnp.concatenate([msg[pl.ds(2 * slot, 1), :], msg[pl.ds(2 * slot + 1, 1), :]], axis=1)
-        ids = jnp.maximum(lab[slot], lab_c[slot])
-        labels = jnp.concatenate([ids[0:1, :], ids[1:2, :]], axis=1).astype(jnp.int32)
-        hot = lax.broadcasted_iota(jnp.int32, (512, PLANE), 0) == labels - base
-        p = jnp.exp(lt_ref[slot] - lse) - jnp.where(hot, 1.0, 0.0)
-        d_ref[:, pl.ds(pl.multiple_of(slot * PLANE, PLANE), PLANE)] = p.astype(jnp.bfloat16)
+        ids = jnp.maximum(lab[slot], lab_c[slot]).astype(jnp.int32) - base
+        for i in range(2):
+            hot = lax.broadcasted_iota(jnp.int32, (512, 128), 0) == ids[i : i + 1, :]
+            p = jnp.exp(lt_ref[i, slot] - fin[i, pl.ds(slot, 1), :]) - jnp.where(hot, 1.0, 0.0)
+            at = pl.multiple_of(slot * PLANE + i * 128, 128)
+            d_ref[:, pl.ds(at, 128)] = p.astype(jnp.bfloat16)
         return carry
 
     lax.fori_loop(0, 8, delta, 0)
     a_copy.wait()
 
+    w_sibling.wait_send()
     for q in range(PIECES):
         for i in range(2):
             @pl.when(jnp.logical_and(holder, jnp.logical_not(jnp.logical_and(mine, c == i))))
@@ -376,10 +421,10 @@
             to_z(slot, slot, q, up_dev).wait_send()
     for s in range(5):
         m = 2 if 0 < s < 4 else 1
+        to_sibling(s, m).wait()
         for i in range(4):
             to_xy(s, m, i, mine_at).wait_send()
             to_diag(s, m, i, mine_at).wait_send()
-            to_sibling(s, m, i).wait_send()
 
 
 def gather(offset, features, labels, other, weight, accum):
@@ -401,25 +446,26 @@
         scratch_shapes=[
             pltpu.VMEM((1, 64), jnp.int32),
             pltpu.VMEM((16, LANES), f32),
-            pltpu.VMEM((8, 512, PLANE), f32),
-            pltpu.VMEM((16, LANES), f32),
-            pltpu.VMEM((15, 16, LANES), f32),
-            pltpu.VMEM((16, LANES), f32),
-            pltpu.VMEM((7, 16, LANES), f32),
-            pltpu.VMEM((16, LANES), f32),
-            pltpu.VMEM((1, 16, LANES), f32),
+            pltpu.VMEM((2, 8, 512, 128), f32),
+            pltpu.VMEM((8, LANES), f32),
+            pltpu.VMEM((15, 8, LANES), f32),
+            pltpu.VMEM((8, LANES), f32),
+            pltpu.VMEM((7, 8, LANES), f32),
+            pltpu.VMEM((2, 8, LANES), f32),
             pltpu.VMEM((8, 2, LANES), f32),
             pltpu.VMEM((15, 2, LANES), f32),
             pltpu.VMEM((8, 2, LANES), f32),
             pltpu.VMEM((64, 2048), jnp.bfloat16),
+            pltpu.VMEM((512, 2048), jnp.bfloat16),
+            pltpu.VMEM((8, 512, 128), f32),
             dma, dma, dma((3,)), dma((PIECES,)), dma((PIECES,)), dma((2, PIECES)),
             dma((8, PIECES)), dma((8, PIECES)),
-            dma((4, 5)), dma((4, 5)), dma((4, 5)), dma((4, 5)), dma((4, 5)), dma((4, 5)),
-            dma((15,)), dma((15,)), dma((7,)), dma((7,)), dma((1,)), dma((1,)),
+            dma((4, 5)), dma((4, 5)), dma((4, 5)), dma((4, 5)), dma((5,)), dma((5,)),
             dma((15,)), dma((15,)), dma((7,)), dma((7,)), dma, dma,
+            dma((15,)), dma((15,)), dma((7,)), dma((7,)), dma, dma, dma, dma, dma((5,)), dma((5,)),
         ],
         compiler_params=pltpu.CompilerParams(
-            collective_id=0, has_side_effects=True, vmem_limit_bytes=16 << 20
+            collective_id=0, has_side_effects=True, vmem_limit_bytes=20 << 20
         ),
     )(offset, *(pltpu.with_memory_space_constraint(v, pltpu.HBM) for v in (features, labels, other, weight, accum)))
 

time: 64 us -> 63.5 us (level)
  no operation moved by 1% of the time
where the time goes in v4:
time: 63.5 us; the launch traced here: 63.4 us
  Pallas kernels  62.2 us (98%)
  between operations  1.28 us (2%)
    pallas_call x1, Pallas kernels, gather(): pl.pallas_call(gather_kernel, out_shape=(jax.ShapeDtypeStruct((8, PLANE,...  55.4 us
    pallas_call x1, Pallas kernels, update(): pl.pallas_call(update_kernel, out_shape=(jax.ShapeDtypeStruct((512, 2048)...  6.78 us

profile of v4, /device:TPU:1, one launch (start us, length us, event | category | flops | bytes accessed | tf_op | source)
XLA Modules:
  0.0 63.4 jit_solution(11899179898515967576)
XLA Ops:
  1.3 55.4 %shard_map.85 = (bf16[8,256,2048]{2,1,0:T(8,128)(2,1)S(1)}, bf16[512,2048]{1,0:T(8,128)(2,1)S(1)}, bf16[512,2048]{1,0:T(8,128)(2,1)S(1)}, f32[512,2048]{1,0:T(8,128)S(1)}, f32[1,64]{1,0:T(1,128)S(1)}) custom-call(s32[1]{0:T(128)S(6)} %copy.9.off_ref, bf16[64,2048]{1,0:T(8,128)(2,1)} %feat_hbm.1, s32[1,64]{1,0:T(1,128)} %bitcast.6, f32[16,128]{1,0:T(8,128)} %bitcast.5, ...), custom_call_target="tpu_custom_call" | custom-call | tf_op jit(solution)/shard_map/pallas_call | solution.py:435
  56.7 6.8 %shard_map.86 = (bf16[512,2048]{1,0:T(8,128)(2,1)}, f32[512,2048]{1,0:T(8,128)}, f32[1,64]{1,0:T(1,128)}) custom-call(bf16[512,2048]{1,0:T(8,128)(2,1)S(1)} %get-tuple-element.11.d_ref, bf16[2048,2048]{1,0:T(8,128)(2,1)S(1)} %bitcast.4, bf16[512,2048]{1,0:T(8,128)(2,1)S(1)} %get-tuple-element.13.w_ref, f32[512,2048]{1,0:T(8,128)S(1)} %get-tuple-element.14.a_ref, ...), custom_call_target="tpu_custom_call" | custom-call | tf_op jit(solution)/shard_map/pallas_call | solution.py:507

commit v5 on v4

--- a/solution.py
+++ b/solution.py
@@ -74,7 +74,7 @@
     diag_devs = [device(i, j, z, c) for j in (yr, yl) for i in (xr, xl)]
 
     plane_peers = [
-        device(rem(x + i // 4, X), rem(y + i % 4, Y), z, c) for i in range(1, 16)
+        device(rem(x + i // 4, X), rem(y + i % 4, Y), z, c) for i in (10, 6, 14, 9, 11, 2, 8, 5, 7, 13, 15, 1, 3, 4, 12)
     ]
     z_peers = [device(x, y, rem(z + i, Z), c) for i in range(1, 8)]
 

time: 63.5 us -> 63.5 us (level)
  no operation moved by 1% of the time
where the time goes in v5:
time: 63.5 us; the launch traced here: 63.4 us
  Pallas kernels  62.1 us (98%)
  between operations  1.28 us (2%)
    pallas_call x1, Pallas kernels, gather(): pl.pallas_call(gather_kernel, out_shape=(jax.ShapeDtypeStruct((8, PLANE,...  55.3 us
    pallas_call x1, Pallas kernels, update(): pl.pallas_call(update_kernel, out_shape=(jax.ShapeDtypeStruct((512, 2048)...  6.78 us

profile of v5, /device:TPU:1, one launch (start us, length us, event | category | flops | bytes accessed | tf_op | source)
XLA Modules:
  0.0 63.4 jit_solution(8299188371486119391)
XLA Ops:
  1.3 55.3 %shard_map.85 = (bf16[8,256,2048]{2,1,0:T(8,128)(2,1)S(1)}, bf16[512,2048]{1,0:T(8,128)(2,1)S(1)}, bf16[512,2048]{1,0:T(8,128)(2,1)S(1)}, f32[512,2048]{1,0:T(8,128)S(1)}, f32[1,64]{1,0:T(1,128)S(1)}) custom-call(s32[1]{0:T(128)S(6)} %copy.9.off_ref, bf16[64,2048]{1,0:T(8,128)(2,1)} %feat_hbm.1, s32[1,64]{1,0:T(1,128)} %bitcast.6, f32[16,128]{1,0:T(8,128)} %bitcast.5, ...), custom_call_target="tpu_custom_call" | custom-call | tf_op jit(solution)/shard_map/pallas_call | solution.py:435
  56.6 6.8 %shard_map.86 = (bf16[512,2048]{1,0:T(8,128)(2,1)}, f32[512,2048]{1,0:T(8,128)}, f32[1,64]{1,0:T(1,128)}) custom-call(bf16[512,2048]{1,0:T(8,128)(2,1)S(1)} %get-tuple-element.11.d_ref, bf16[2048,2048]{1,0:T(8,128)(2,1)S(1)} %bitcast.4, bf16[512,2048]{1,0:T(8,128)(2,1)S(1)} %get-tuple-element.13.w_ref, f32[512,2048]{1,0:T(8,128)S(1)} %get-tuple-element.14.a_ref, ...), custom_call_target="tpu_custom_call" | custom-call | tf_op jit(solution)/shard_map/pallas_call | solution.py:507
